TPU v7x, 32 devices: a whole 2x2x4 slice. The times are simulated.
32 devices in a mesh: seq: 16 (over z, x, core), head: 2 (over y).
Axes of the slice: x: 2, y: 2, z: 4, core: 2. Of those that a mesh axis runs over, the one named last changes fastest.
Arguments:
- points: bfloat16 [16384, 512], P(('seq', 'head')), may hold values from -5000 to 5000
- norm_gain: float32 [512], replicated, may hold values from 0.1 to 1.9
- qkv_weight: bfloat16 [3, 512, 512], replicated, may hold values from -24 to 24
- out_weight: bfloat16 [512, 512], replicated, may hold values from -4 to 4
- neighbours: int32 [64, 8], replicated, may hold values from 0 to 63, as said below
Outputs:
- update: bfloat16 [16384, 512], P(('seq', 'head'))
Inputs may be any that keep to these rules, and one draw needn't show every extreme that they name: `neighbours`: column 0 of row p is p. Columns 1 to 4 are distinct patches p + s with 0 < |s| <= 4. The last 3 columns name patches whose owner (patch // 4) is not the owner of p. Over all patches of one owner, the far columns name any one other owner at most 1 times, each time a different patch, and every owner reaches 1 with some other owner.
All inputs are finite; a program needn't handle non-finite values.
Results may differ from a plain program's by a relative error of at most 0.006.
The roundings to bfloat16 on the way count: a program that leaves them out, or rounds other values in their place, can miss the bound.
Values may be sent and summed in bfloat16 or wider, within the bound.
No kernel may reach another device: no remote copies, remote signals or barrier semaphores. Data moves between devices by JAX's collectives and lax.ppermute only.
A program may use at most 64 MiB of HBM per device.

v0:
```python
import jax
import jax.numpy as jnp
from jax import lax
from jax.sharding import PartitionSpec as P

D = 512
HEAD_DIM = 32
PATCH = 256
NEIGH = 8
NEAR = 4
FAR = 3
EPS = 1e-06


def with_halo(cells, sides, width):
    for axis, dim in sides:
        count = lax.axis_size(axis)
        ends = count - 1
        head = lax.slice_in_dim(cells, 0, width, axis=dim)
        tail = lax.slice_in_dim(cells, cells.shape[dim] - width, cells.shape[dim], axis=dim)
        cells = jnp.concatenate(
            [
                lax.ppermute(tail, axis, [(i, (i + 1) % count) for i in range(ends)]),
                cells,
                lax.ppermute(head, axis, [((i + 1) % count, i) for i in range(ends)]),
            ],
            axis=dim,
        )
    return cells


def attend_patch(operands):
    query_rows, kv_rows = operands
    local_width = query_rows.shape[1]
    local_heads = local_width // HEAD_DIM
    query_rows = query_rows.reshape(PATCH, local_heads, HEAD_DIM)
    key_rows = kv_rows[:, :local_width].reshape(-1, local_heads, HEAD_DIM)
    values = kv_rows[:, local_width:].reshape(-1, local_heads, HEAD_DIM)
    scores = jnp.einsum(
        "qhd,khd->hqk", query_rows, key_rows, preferred_element_type=jnp.float32
    ) * HEAD_DIM ** (-0.5)
    row_top = jnp.max(scores, axis=2, keepdims=True)
    lifted = jnp.exp(scores - row_top)
    weights = (lifted / jnp.sum(lifted, axis=2, keepdims=True)).astype(jnp.bfloat16)
    mixed_rows = jnp.einsum("hqk,khd->qhd", weights, values, preferred_element_type=jnp.float32)
    return mixed_rows.astype(jnp.bfloat16).reshape(PATCH, local_width)


def body(points, norm_gain, qkv_weight, out_weight, neighbours):
    head_count = lax.axis_size("head")
    head_index = lax.axis_index("head")
    seq_count = lax.axis_size("seq")
    shard_index = lax.axis_index("seq")
    column_share = D // head_count
    floats = points.astype(jnp.float32)
    mean_square = jnp.sum(floats * floats, axis=1, keepdims=True) / D
    normed = (floats * lax.rsqrt(mean_square + EPS) * norm_gain).astype(jnp.bfloat16)
    grouped_weight = (
        qkv_weight.reshape(3, D, head_count, column_share)
        .transpose(1, 2, 0, 3)
        .reshape(D, head_count, 3 * column_share)
    )
    own_columns = lax.dynamic_index_in_dim(grouped_weight, head_index, 1, keepdims=False)
    projected = jnp.dot(
        lax.all_gather(normed, "head", axis=0, tiled=True),
        own_columns,
        preferred_element_type=jnp.float32,
    ).astype(jnp.bfloat16)
    row_count = projected.shape[0]
    per_shard = row_count // PATCH
    queries = projected[:, :column_share]
    kv_local = projected[:, column_share:].reshape(per_shard, PATCH, 2 * column_share)
    extended = with_halo(kv_local, (("seq", 0),), per_shard)
    own_lists = lax.dynamic_slice_in_dim(neighbours, shard_index * per_shard, per_shard, 0)
    near_index = own_lists[:, : 1 + NEAR] - (shard_index - 1) * per_shard
    near_rows = extended[near_index]
    ref_count = per_shard * FAR
    far_lists = neighbours[:, 1 + NEAR :].reshape(seq_count, ref_count)
    owners = far_lists // per_shard
    local_ids = far_lists % per_shard
    earlier = jnp.arange(ref_count)[None, :] < jnp.arange(ref_count)[:, None]
    same_owner = owners[:, :, None] == owners[:, None, :]
    slot_ranks = jnp.sum(same_owner & earlier[None], axis=2)
    slot_count = (FAR * per_shard + seq_count - 2) // (seq_count - 1)
    owned_refs = (owners == shard_index).astype(jnp.float32)
    slot_hot = (slot_ranks[:, :, None] == jnp.arange(slot_count)[None, None, :]).astype(jnp.float32)
    local_hot = (local_ids[:, :, None] == jnp.arange(per_shard)[None, None, :]).astype(jnp.float32)
    selector = jnp.einsum("rk,rkj,rkl->rjl", owned_refs, slot_hot, local_hot).astype(jnp.bfloat16)
    flat_kv = kv_local.reshape(per_shard, PATCH * 2 * column_share)
    outgoing = jnp.dot(
        selector.reshape(seq_count * slot_count, per_shard),
        flat_kv,
        preferred_element_type=jnp.float32,
    )
    outgoing = outgoing.astype(jnp.bfloat16).reshape(seq_count, slot_count, PATCH, 2 * column_share)
    incoming = lax.all_to_all(outgoing, "seq", split_axis=0, concat_axis=0, tiled=True)
    my_owners = lax.dynamic_index_in_dim(owners, shard_index, 0, keepdims=False)
    my_slots = lax.dynamic_index_in_dim(slot_ranks, shard_index, 0, keepdims=False)
    far_rows = incoming.reshape(seq_count * slot_count, PATCH, 2 * column_share)[
        my_owners * slot_count + my_slots
    ]
    far_rows = far_rows.reshape(per_shard, FAR, PATCH, 2 * column_share)
    gathered = jnp.concatenate([near_rows, far_rows], axis=1).reshape(
        per_shard, NEIGH * PATCH, 2 * column_share
    )
    attended = lax.map(
        attend_patch, (queries.reshape(per_shard, PATCH, column_share), gathered)
    ).reshape(row_count, column_share)
    owned_rows = lax.all_to_all(attended, "head", split_axis=0, concat_axis=1, tiled=True)
    update = jnp.dot(owned_rows, out_weight, preferred_element_type=jnp.float32).astype(
        jnp.bfloat16
    )
    return update


def solution(mesh):
    placed = (P(("seq", "head"), None), P(), P(), P(), P())
    return jax.shard_map(
        body, mesh=mesh, in_specs=placed, out_specs=P(("seq", "head"), None), check_vma=False
    )
```

profile of v0, /device:TPU:16, one launch (start us, length us, event | category | flops | bytes accessed | tf_op | source)
XLA Modules:
  0.0 306.8 jit_solution(17444510389994302412)
XLA Ops:
  7.8 2.0 fusion.12
  14.0 18.4 %all-gather.2.cloned.1.call-done = bf16[1024,512]{1,0:T(8,128)(2,1)} async-done(((bf16[512,512]{1,0:T(8,128)(2,1)}), bf16[1024,512]{1,0:T(8,128)(2,1)}) %all-gather.2.cloned.1.call-update) | async-done | bytes 1048592 | tf_op jit(solution)/shard_map/all_gather | solution.py:65
  32.4 2.5 convolution_convert_fusion.1
  38.2 3.5 %copy.78 = bf16[2,8,256,512]{3,2,1,0:T(8,128)(2,1)} copy(bf16[2,8,256,512]{3,1,2,0:T(8,128)(2,1)S(1)} %bitcast.71) | data formatting | bytes 8388608
  41.7 6.0 %all-to-all-start = ((bf16[16,1,256,512]{3,2,1,0:T(8,128)(2,1)}), bf16[16,1,256,512]{3,2,1,0:T(8,128)(2,1)}, u32[]{:S(2)}, u32[]{:S(2)}) async-start(bf16[16,1,256,512]{3,2,1,0:T(8,128)(2,1)} %bitcast.72), calls=%async_computation | async-start | bytes 8388608 | tf_op jit(solution)/shard_map/all_to_all | solution.py:96
  49.8 4.6 %collective-permute-start.1 = (bf16[4,256,512]{2,1,0:T(8,128)(2,1)S(1)}, bf16[4,256,512]{2,1,0:T(8,128)(2,1)}, u32[]{:S(2)}, u32[]{:S(2)}) collective-permute-start(bf16[4,256,512]{2,1,0:T(8,128)(2,1)S(1)} %bitcast.75), channel_id=1, source_target_pairs={{2,0},{4,2},{6,4},{8,6},{10,8},{12,10},{14,12},{16,14},{18,16},{20... | collective-permute-start | bytes 3145736 | tf_op jit(solution)/shard_map/ppermute | solution.py:25
  54.9 96.6 %collective-permute-done = bf16[4,256,512]{2,1,0:T(8,128)(2,1)S(1)} collective-permute-done((bf16[4,256,512]{2,1,0:T(8,128)(2,1)S(1)}, bf16[4,256,512]{2,1,0:T(8,128)(2,1)S(1)}, u32[]{:S(2)}, u32[]{:S(2)}) %collective-permute-start) | collective-permute-done | bytes 1048608 | tf_op jit(solution)/shard_map/ppermute | solution.py:23
  151.6 2.8 pad_maximum_fusion.1
  154.4 6.1 %gather_fusion = bf16[20,256,512]{2,1,0:T(8,128)(2,1)} fusion(bf16[12,256,512]{2,1,0:T(8,128)(2,1)} %pad_maximum_fusion.1, s32[1024]{0:T(1024)S(1)} %pad_clamp_fusion.1), kind=kCustom, calls=%fused_computation | custom fusion | bytes 10485840 | tf_op jit(solution)/shard_map/gather | solution.py:76
  160.5 13.8 %copy.68 = bf16[4,5,256,512]{2,1,3,0:T(8,128)(2,1)} copy(bf16[4,5,256,512]{3,2,1,0:T(8,128)(2,1)} %bitcast.70) | data formatting | bytes 10485760 | tf_op jit(solution)/shard_map/gather | solution.py:76
  174.3 4.8 %gather_fusion.1 = bf16[12,256,512]{2,1,0:T(8,128)(2,1)} fusion(bf16[16,256,512]{2,1,0:T(8,128)(2,1)} %bitcast.16, s32[1024]{0:T(1024)S(1)} %pad_clamp_fusion), kind=kCustom, calls=%fused_computation.1 | custom fusion | bytes 6291504 | tf_op jit(solution)/shard_map/gather | solution.py:99
  179.1 7.1 %copy.69 = bf16[4,3,256,512]{2,1,3,0:T(4,128)(2,1)} copy(bf16[4,3,256,512]{3,2,1,0:T(8,128)(2,1)} %bitcast.73) | data formatting | bytes 6291456 | tf_op jit(solution)/shard_map/reshape | solution.py:102
  186.2 9.7 %pad_maximum_fusion = bf16[4,8,256,512]{2,1,3,0:T(8,128)(2,1)} fusion(bf16[4,3,256,512]{2,1,3,0:T(4,128)(2,1)} %copy.69, bf16[4,5,256,512]{2,1,3,0:T(8,128)(2,1)} %copy.68), kind=kLoop, calls=%fused_computation.16 | loop fusion | flops 16777216 | bytes 16777216 | tf_op jit(solution)/shard_map/concatenate | solution.py:103
  196.0 13.5 %reshape.188 = bf16[4,2048,512]{1,2,0:T(8,128)(2,1)} reshape(bf16[4,8,256,512]{2,1,3,0:T(8,128)(2,1)} %pad_maximum_fusion) | data formatting | bytes 16777216 | tf_op jit(solution)/shard_map/reshape | solution.py:103
  209.5 79.0 %while.10 = (s32[]{:T(128)}, bf16[4,256,256]{2,1,0:T(8,128)(2,1)}, bf16[4,2048,512]{1,2,0:T(8,128)(2,1)}, bf16[4,256,256]{2,1,0:T(8,128)(2,1)S(1)}, s32[]{:T(128)}) while((s32[]{:T(128)}, bf16[4,256,256]{2,1,0:T(8,128)(2,1)}, bf16[4,2048,512]{1,2,0:T(8,128)(2,1)}, bf16[4,256,256]{2,1,0:T(8,128)(2,1)S(1)}, s32[]{:T(128)}) %tuple.36), condition=%wide.region_5.6_spmd, body=%wide.region_2.5_spmd.sunk | while | flops 557910016 | bytes 45367876 | solution.py:106
  211.5 8.5 %fusion.44 = (f32[8,256]{1,0:T(8,128)S(1)}, f32[8,256,2048]{2,1,0:T(8,128)}) fusion(bf16[256,8,32]{0,2,1:T(8,128)(2,1)S(1)} %bitcast.78, bf16[2048,8,32]{0,2,1:T(8,128)(2,1)S(1)} %bitcast.69), kind=kOutput, calls=%fused_computation.52.clone.1 | convolution fusion | flops 281020416 | bytes 17965056 | tf_op jit(solution)/shard_map/while/body/eval_jaxpr/sub | solution.py:43
  220.0 8.5 %fusion.45 = bf16[8,32,256]{2,1,0:T(8,128)(2,1)S(1)} fusion(bf16[2048,8,32]{0,2,1:T(8,128)(2,1)S(1)} %bitcast.68, f32[8,256,2048]{2,1,0:T(8,128)} %get-tuple-element.97, f32[8,256]{1,0:T(8,128)S(1)} %get-tuple-element.98), kind=kOutput, calls=%fused_computation.11.clone.1 | convolution fusion | flops 276889600 | bytes 17965056 | tf_op jit(solution)/shard_map/while/body/eval_jaxpr/hqk,khd->qhd/dot_general | solution.py:45
  231.2 8.5 %fusion.44 = (f32[8,256]{1,0:T(8,128)S(1)}, f32[8,256,2048]{2,1,0:T(8,128)}) fusion(bf16[256,8,32]{0,2,1:T(8,128)(2,1)S(1)} %bitcast.78, bf16[2048,8,32]{0,2,1:T(8,128)(2,1)S(1)} %bitcast.69), kind=kOutput, calls=%fused_computation.52.clone.1 | convolution fusion | flops 281020416 | bytes 17965056 | tf_op jit(solution)/shard_map/while/body/eval_jaxpr/sub | solution.py:43
  239.7 8.5 %fusion.45 = bf16[8,32,256]{2,1,0:T(8,128)(2,1)S(1)} fusion(bf16[2048,8,32]{0,2,1:T(8,128)(2,1)S(1)} %bitcast.68, f32[8,256,2048]{2,1,0:T(8,128)} %get-tuple-element.97, f32[8,256]{1,0:T(8,128)S(1)} %get-tuple-element.98), kind=kOutput, calls=%fused_computation.11.clone.1 | convolution fusion | flops 276889600 | bytes 17965056 | tf_op jit(solution)/shard_map/while/body/eval_jaxpr/hqk,khd->qhd/dot_general | solution.py:45
  251.0 8.5 %fusion.44 = (f32[8,256]{1,0:T(8,128)S(1)}, f32[8,256,2048]{2,1,0:T(8,128)}) fusion(bf16[256,8,32]{0,2,1:T(8,128)(2,1)S(1)} %bitcast.78, bf16[2048,8,32]{0,2,1:T(8,128)(2,1)S(1)} %bitcast.69), kind=kOutput, calls=%fused_computation.52.clone.1 | convolution fusion | flops 281020416 | bytes 17965056 | tf_op jit(solution)/shard_map/while/body/eval_jaxpr/sub | solution.py:43
  259.5 8.5 %fusion.45 = bf16[8,32,256]{2,1,0:T(8,128)(2,1)S(1)} fusion(bf16[2048,8,32]{0,2,1:T(8,128)(2,1)S(1)} %bitcast.68, f32[8,256,2048]{2,1,0:T(8,128)} %get-tuple-element.97, f32[8,256]{1,0:T(8,128)S(1)} %get-tuple-element.98), kind=kOutput, calls=%fused_computation.11.clone.1 | convolution fusion | flops 276889600 | bytes 17965056 | tf_op jit(solution)/shard_map/while/body/eval_jaxpr/hqk,khd->qhd/dot_general | solution.py:45
  270.7 8.5 %fusion.44 = (f32[8,256]{1,0:T(8,128)S(1)}, f32[8,256,2048]{2,1,0:T(8,128)}) fusion(bf16[256,8,32]{0,2,1:T(8,128)(2,1)S(1)} %bitcast.78, bf16[2048,8,32]{0,2,1:T(8,128)(2,1)S(1)} %bitcast.69), kind=kOutput, calls=%fused_computation.52.clone.1 | convolution fusion | flops 281020416 | bytes 17965056 | tf_op jit(solution)/shard_map/while/body/eval_jaxpr/sub | solution.py:43
  279.2 8.5 %fusion.45 = bf16[8,32,256]{2,1,0:T(8,128)(2,1)S(1)} fusion(bf16[2048,8,32]{0,2,1:T(8,128)(2,1)S(1)} %bitcast.68, f32[8,256,2048]{2,1,0:T(8,128)} %get-tuple-element.97, f32[8,256]{1,0:T(8,128)S(1)} %get-tuple-element.98), kind=kOutput, calls=%fused_computation.11.clone.1 | convolution fusion | flops 276889600 | bytes 17965056 | tf_op jit(solution)/shard_map/while/body/eval_jaxpr/hqk,khd->qhd/dot_general | solution.py:45
  288.5 10.1 %all_to_all.24 = bf16[2,512,256]{2,1,0:T(8,128)(2,1)S(1)} all-to-all(bf16[2,512,256]{2,1,0:T(8,128)(2,1)} %bitcast.83), channel_id=1, replica_groups=mesh['seq'=16,'head'=2] {'head'}, dimensions={0} | all-to-all | bytes 1048576 | tf_op jit(solution)/shard_map/all_to_all | solution.py:109
  (67 shorter events, 23.7 us)
Async XLA Ops:
  6.5 292.2 %copy-start = (bf16[512,512]{1,0:T(8,128)(2,1)S(1)}, bf16[512,512]{1,0:T(8,128)(2,1)}, u32[]{:S(2)}) copy-start(bf16[512,512]{1,0:T(8,128)(2,1)} %param.10) | copy-start | bytes 1572868
  6.5 6.4 %copy-start.2 = (s32[64,8]{0,1:T(8,128)S(1)}, s32[64,8]{0,1:T(8,128)}, u32[]{:S(2)}) copy-start(s32[64,8]{0,1:T(8,128)} %param.11) | copy-start | bytes 6148
  6.5 25.9 %all-gather.2.cloned.1.call-start = ((), (), s32[]{:S(2)}) async-start(), calls=%async_computation.2 | async-start | bytes 1572864 | tf_op jit(solution)/shard_map/all_gather | solution.py:65
  34.9 1.2 copy-start.1
  41.7 132.6 %all-to-all-start = ((bf16[16,1,256,512]{3,2,1,0:T(8,128)(2,1)}), bf16[16,1,256,512]{3,2,1,0:T(8,128)(2,1)}, u32[]{:S(2)}, u32[]{:S(2)}) async-start(bf16[16,1,256,512]{3,2,1,0:T(8,128)(2,1)} %bitcast.72), calls=%async_computation | async-start | bytes 8388608 | tf_op jit(solution)/shard_map/all_to_all | solution.py:96
  47.8 103.8 %collective-permute-start = (bf16[4,256,512]{2,1,0:T(8,128)(2,1)S(1)}, bf16[4,256,512]{2,1,0:T(8,128)(2,1)S(1)}, u32[]{:S(2)}, u32[]{:S(2)}) collective-permute-start(bf16[4,256,512]{2,1,0:T(8,128)(2,1)S(1)} %bitcast.74), channel_id=1, source_target_pairs={{0,2},{2,4},{4,6},{6,8},{8,10},{10,12},{12,14},{14,16},{16,18},{18... | collective-permute-start | bytes 3145736 | tf_op jit(solution)/shard_map/ppermute | solution.py:23
  49.8 101.8 %collective-permute-start.1 = (bf16[4,256,512]{2,1,0:T(8,128)(2,1)S(1)}, bf16[4,256,512]{2,1,0:T(8,128)(2,1)}, u32[]{:S(2)}, u32[]{:S(2)}) collective-permute-start(bf16[4,256,512]{2,1,0:T(8,128)(2,1)S(1)} %bitcast.75), channel_id=1, source_target_pairs={{2,0},{4,2},{6,4},{8,6},{10,8},{12,10},{14,12},{16,14},{18,16},{20... | collective-permute-start | bytes 3145736 | tf_op jit(solution)/shard_map/ppermute | solution.py:25
  196.0 13.5 %slice-start = ((bf16[1024,768]{1,0:T(8,128)(2,1)}), bf16[1024,256]{1,0:T(8,128)(2,1)S(1)}, s32[]{:S(2)}) async-start(bf16[1024,768]{1,0:T(8,128)(2,1)} %copy-done.1), calls=%async_computation.3 | async-start | bytes 1048576 | tf_op jit(solution)/shard_map/slice | solution.py:71
Sparse Core Ops, SparseCore 0:
  10.0 22.3 all-gather.1
where the time goes:
time: 308 us; the launch traced here: 307 us
  waiting for transfers between devices  115 us (37%)
  matrix products  72.9 us (24%)
  local copies, waits for them, and re-layouts  66 us (21%)
  other arithmetic  16.5 us (5%)
  between operations  13.5 us (4%)
  starting transfers between devices  12.7 us (4%)
  blocking collectives  10.1 us (3%)
    ppermute x1, waiting for transfers between devices, with_halo(): lax.ppermute(tail, axis, [(i, (i + 1) % count) for i in range(ends)])  96.6 us
    sub x4, matrix products, attend_patch(): lifted = jnp.exp(scores - row_top)  33.9 us
    dot_general x4, matrix products, attend_patch(): jnp.einsum('hqk,khd->qhd', weights, values, preferred_element_type=jnp.fl...  33.8 us
    gather x2, local copies, waits for them, and re-layouts, body(): near_rows = extended[near_index]  19.9 us
    all_gather x1, waiting for transfers between devices, body(): lax.all_gather(normed, 'head', axis=0, tiled=True)  18.4 us
    reshape x1, local copies, waits for them, and re-layouts, body(): jnp.concatenate([near_rows, far_rows], axis=1)  13.5 us
    all_to_all x1, blocking collectives, body(): lax.all_to_all(attended, 'head', split_axis=0, concat_axis=1, tiled=True)  10.1 us
    concatenate x1, other arithmetic, body(): jnp.concatenate([near_rows, far_rows], axis=1)  9.73 us
  transfers between devices with their start and end apart: 4, of which 2 were waited for; matrix products, arithmetic and copies ran while one was open for 9% of the time, Pallas kernels for 0%

commit v1 on v0

--- a/solution.py
+++ b/solution.py
@@ -10,6 +10,28 @@
 NEAR = 4
 FAR = 3
 EPS = 1e-06
+
+
+def joined_along(pieces, dim):
+    shape = list(pieces.shape[1:])
+    shape[dim] *= pieces.shape[0]
+    return jnp.moveaxis(pieces, 0, dim).reshape(shape)
+
+
+def doubled(shard, axis):
+    size = lax.axis_size(axis)
+    blocks = shard[None]
+    for level in range(size.bit_length() - 1):
+        bit = 1 << level
+        partner_block = lax.ppermute(blocks, axis, [(i, i ^ bit) for i in range(size)])
+        both = jnp.stack([blocks, partner_block])
+        upper = lax.axis_index(axis) >> level & 1
+        blocks = jnp.where(upper == 0, both, both[::-1]).reshape(-1, *shard.shape)
+    return blocks
+
+
+def collect(x, axis, dim):
+    return joined_along(doubled(x, axis), dim)
 
 
 def with_halo(cells, sides, width):
@@ -62,9 +84,7 @@
     )
     own_columns = lax.dynamic_index_in_dim(grouped_weight, head_index, 1, keepdims=False)
     projected = jnp.dot(
-        lax.all_gather(normed, "head", axis=0, tiled=True),
-        own_columns,
-        preferred_element_type=jnp.float32,
+        collect(normed, "head", 0), own_columns, preferred_element_type=jnp.float32
     ).astype(jnp.bfloat16)
     row_count = projected.shape[0]
     per_shard = row_count // PATCH

time: 308 us -> 287 us (0.932)
  between operations: 13.5 us -> 0.17 us
  waiting for transfers between devices: 115 us -> 105 us
    all_gather x1 -> x0, waiting for transfers between devices: 18.4 us -> none  [body(): lax.all_gather(normed, 'head', axis=0, tiled=True)]
    ppermute x0 -> x1, waiting for transfers between devices: none -> 8.12 us  [doubled(): lax.ppermute(blocks, axis, [(i, i ^ bit) for i in range(size)])]
  transfers between devices with their start and end apart: 4 -> 4, of which waited for: 2 -> 2; matrix products, arithmetic and copies ran while one was open for 9% -> 10% of each run, Pallas kernels for 0% -> 0%
where the time goes in v1:
time: 287 us; the launch traced here: 285 us
  waiting for transfers between devices  105 us (37%)
  matrix products  72.6 us (25%)
  local copies, waits for them, and re-layouts  66.1 us (23%)
  other arithmetic  17 us (6%)
  starting transfers between devices  14.4 us (5%)
  blocking collectives  10.1 us (4%)
    ppermute x1, waiting for transfers between devices, with_halo(): lax.ppermute(tail, axis, [(i, (i + 1) % count) for i in range(ends)])  96.6 us
    sub x4, matrix products, attend_patch(): lifted = jnp.exp(scores - row_top)  33.9 us
    dot_general x4, matrix products, attend_patch(): jnp.einsum('hqk,khd->qhd', weights, values, preferred_element_type=jnp.fl...  33.8 us
    gather x2, local copies, waits for them, and re-layouts, body(): near_rows = extended[near_index]  19.9 us
    reshape x1, local copies, waits for them, and re-layouts, body(): jnp.concatenate([near_rows, far_rows], axis=1)  13.5 us
    all_to_all x1, blocking collectives, body(): lax.all_to_all(attended, 'head', split_axis=0, concat_axis=1, tiled=True)  10.1 us
    concatenate x1, other arithmetic, body(): jnp.concatenate([near_rows, far_rows], axis=1)  9.73 us
    ppermute x1, waiting for transfers between devices, doubled(): lax.ppermute(blocks, axis, [(i, i ^ bit) for i in range(size)])  8.12 us
  transfers between devices with their start and end apart: 4, of which 2 were waited for; matrix products, arithmetic and copies ran while one was open for 10% of the time, Pallas kernels for 0%

profile of v1, /device:TPU:16, one launch (start us, length us, event | category | flops | bytes accessed | tf_op | source)
XLA Modules:
  0.0 285.2 jit_solution(1511712126649864077)
XLA Ops:
  8.3 8.1 %collective-permute-done = bf16[1,512,512]{2,1,0:T(8,128)(2,1)} collective-permute-done((bf16[1,512,512]{2,1,0:T(8,128)(2,1)S(1)}, bf16[1,512,512]{2,1,0:T(8,128)(2,1)}, u32[]{:S(2)}, u32[]{:S(2)}) %collective-permute-start) | collective-permute-done | bytes 524320 | tf_op jit(solution)/shard_map/ppermute | solution.py:26
  17.7 2.2 convolution_convert_fusion.1
  23.2 3.5 %copy.78 = bf16[2,8,256,512]{3,2,1,0:T(8,128)(2,1)} copy(bf16[2,8,256,512]{3,1,2,0:T(8,128)(2,1)S(1)} %bitcast.77) | data formatting | bytes 8388608
  26.7 6.2 %all-to-all-start = ((bf16[16,1,256,512]{3,2,1,0:T(8,128)(2,1)}), bf16[16,1,256,512]{3,2,1,0:T(8,128)(2,1)}, u32[]{:S(2)}, u32[]{:S(2)}) async-start(bf16[16,1,256,512]{3,2,1,0:T(8,128)(2,1)} %bitcast.78), calls=%async_computation | async-start | bytes 8388608 | tf_op jit(solution)/shard_map/all_to_all | solution.py:116
  32.9 2.0 collective-permute-start.1
  34.9 4.6 %collective-permute-start.2 = (bf16[4,256,512]{2,1,0:T(8,128)(2,1)S(1)}, bf16[4,256,512]{2,1,0:T(8,128)(2,1)}, u32[]{:S(2)}, u32[]{:S(2)}) collective-permute-start(bf16[4,256,512]{2,1,0:T(8,128)(2,1)S(1)} %bitcast.81), channel_id=1, source_target_pairs={{2,0},{4,2},{6,4},{8,6},{10,8},{12,10},{14,12},{16,14},{18,16},{20... | collective-permute-start | bytes 3145736 | tf_op jit(solution)/shard_map/ppermute | solution.py:47
  40.1 96.6 %collective-permute-done.1 = bf16[4,256,512]{2,1,0:T(8,128)(2,1)S(1)} collective-permute-done((bf16[4,256,512]{2,1,0:T(8,128)(2,1)S(1)}, bf16[4,256,512]{2,1,0:T(8,128)(2,1)S(1)}, u32[]{:S(2)}, u32[]{:S(2)}) %collective-permute-start.1) | collective-permute-done | bytes 1048608 | tf_op jit(solution)/shard_map/ppermute | solution.py:45
  136.7 2.8 pad_maximum_fusion.1
  139.5 6.1 %gather_fusion = bf16[20,256,512]{2,1,0:T(8,128)(2,1)} fusion(bf16[12,256,512]{2,1,0:T(8,128)(2,1)} %pad_maximum_fusion.1, s32[1024]{0:T(1024)S(1)} %pad_clamp_fusion.1), kind=kCustom, calls=%fused_computation | custom fusion | bytes 10485840 | tf_op jit(solution)/shard_map/gather | solution.py:96
  145.6 13.8 %copy.68 = bf16[4,5,256,512]{2,1,3,0:T(8,128)(2,1)} copy(bf16[4,5,256,512]{3,2,1,0:T(8,128)(2,1)} %bitcast.76) | data formatting | bytes 10485760 | tf_op jit(solution)/shard_map/gather | solution.py:96
  159.4 4.8 %gather_fusion.1 = bf16[12,256,512]{2,1,0:T(8,128)(2,1)} fusion(bf16[16,256,512]{2,1,0:T(8,128)(2,1)} %bitcast.20, s32[1024]{0:T(1024)S(1)} %pad_clamp_fusion), kind=kCustom, calls=%fused_computation.1 | custom fusion | bytes 6291504 | tf_op jit(solution)/shard_map/gather | solution.py:119
  164.3 7.1 %copy.69 = bf16[4,3,256,512]{2,1,3,0:T(4,128)(2,1)} copy(bf16[4,3,256,512]{3,2,1,0:T(8,128)(2,1)} %bitcast.79) | data formatting | bytes 6291456 | tf_op jit(solution)/shard_map/reshape | solution.py:122
  171.4 9.7 %pad_maximum_fusion = bf16[4,8,256,512]{2,1,3,0:T(8,128)(2,1)} fusion(bf16[4,3,256,512]{2,1,3,0:T(4,128)(2,1)} %copy.69, bf16[4,5,256,512]{2,1,3,0:T(8,128)(2,1)} %copy.68), kind=kLoop, calls=%fused_computation.16 | loop fusion | flops 16777216 | bytes 16777216 | tf_op jit(solution)/shard_map/concatenate | solution.py:123
  181.1 13.5 %reshape.188 = bf16[4,2048,512]{1,2,0:T(8,128)(2,1)} reshape(bf16[4,8,256,512]{2,1,3,0:T(8,128)(2,1)} %pad_maximum_fusion) | data formatting | bytes 16777216 | tf_op jit(solution)/shard_map/reshape | solution.py:123
  194.7 79.0 %while.10 = (s32[]{:T(128)}, bf16[4,256,256]{2,1,0:T(8,128)(2,1)}, bf16[4,2048,512]{1,2,0:T(8,128)(2,1)}, bf16[4,256,256]{2,1,0:T(8,128)(2,1)S(1)}, s32[]{:T(128)}) while((s32[]{:T(128)}, bf16[4,256,256]{2,1,0:T(8,128)(2,1)}, bf16[4,2048,512]{1,2,0:T(8,128)(2,1)}, bf16[4,256,256]{2,1,0:T(8,128)(2,1)S(1)}, s32[]{:T(128)}) %tuple.35), condition=%wide.region_5.6_spmd, body=%wide.region_2.5_spmd.sunk | while | flops 557910016 | bytes 45367876 | solution.py:126
  196.7 8.5 %fusion.46 = (f32[8,256]{1,0:T(8,128)S(1)}, f32[8,256,2048]{2,1,0:T(8,128)}) fusion(bf16[256,8,32]{0,2,1:T(8,128)(2,1)S(1)} %bitcast.84, bf16[2048,8,32]{0,2,1:T(8,128)(2,1)S(1)} %bitcast.75), kind=kOutput, calls=%fused_computation.56.clone.1 | convolution fusion | flops 281020416 | bytes 17965056 | tf_op jit(solution)/shard_map/while/body/eval_jaxpr/sub | solution.py:65
  205.2 8.5 %fusion.47 = bf16[8,32,256]{2,1,0:T(8,128)(2,1)S(1)} fusion(bf16[2048,8,32]{0,2,1:T(8,128)(2,1)S(1)} %bitcast.74, f32[8,256,2048]{2,1,0:T(8,128)} %get-tuple-element.99, f32[8,256]{1,0:T(8,128)S(1)} %get-tuple-element.100), kind=kOutput, calls=%fused_computation.11.clone.1 | convolution fusion | flops 276889600 | bytes 17965056 | tf_op jit(solution)/shard_map/while/body/eval_jaxpr/hqk,khd->qhd/dot_general | solution.py:67
  216.4 8.5 %fusion.46 = (f32[8,256]{1,0:T(8,128)S(1)}, f32[8,256,2048]{2,1,0:T(8,128)}) fusion(bf16[256,8,32]{0,2,1:T(8,128)(2,1)S(1)} %bitcast.84, bf16[2048,8,32]{0,2,1:T(8,128)(2,1)S(1)} %bitcast.75), kind=kOutput, calls=%fused_computation.56.clone.1 | convolution fusion | flops 281020416 | bytes 17965056 | tf_op jit(solution)/shard_map/while/body/eval_jaxpr/sub | solution.py:65
  224.9 8.5 %fusion.47 = bf16[8,32,256]{2,1,0:T(8,128)(2,1)S(1)} fusion(bf16[2048,8,32]{0,2,1:T(8,128)(2,1)S(1)} %bitcast.74, f32[8,256,2048]{2,1,0:T(8,128)} %get-tuple-element.99, f32[8,256]{1,0:T(8,128)S(1)} %get-tuple-element.100), kind=kOutput, calls=%fused_computation.11.clone.1 | convolution fusion | flops 276889600 | bytes 17965056 | tf_op jit(solution)/shard_map/while/body/eval_jaxpr/hqk,khd->qhd/dot_general | solution.py:67
  236.2 8.5 %fusion.46 = (f32[8,256]{1,0:T(8,128)S(1)}, f32[8,256,2048]{2,1,0:T(8,128)}) fusion(bf16[256,8,32]{0,2,1:T(8,128)(2,1)S(1)} %bitcast.84, bf16[2048,8,32]{0,2,1:T(8,128)(2,1)S(1)} %bitcast.75), kind=kOutput, calls=%fused_computation.56.clone.1 | convolution fusion | flops 281020416 | bytes 17965056 | tf_op jit(solution)/shard_map/while/body/eval_jaxpr/sub | solution.py:65
  244.7 8.5 %fusion.47 = bf16[8,32,256]{2,1,0:T(8,128)(2,1)S(1)} fusion(bf16[2048,8,32]{0,2,1:T(8,128)(2,1)S(1)} %bitcast.74, f32[8,256,2048]{2,1,0:T(8,128)} %get-tuple-element.99, f32[8,256]{1,0:T(8,128)S(1)} %get-tuple-element.100), kind=kOutput, calls=%fused_computation.11.clone.1 | convolution fusion | flops 276889600 | bytes 17965056 | tf_op jit(solution)/shard_map/while/body/eval_jaxpr/hqk,khd->qhd/dot_general | solution.py:67
  255.9 8.5 %fusion.46 = (f32[8,256]{1,0:T(8,128)S(1)}, f32[8,256,2048]{2,1,0:T(8,128)}) fusion(bf16[256,8,32]{0,2,1:T(8,128)(2,1)S(1)} %bitcast.84, bf16[2048,8,32]{0,2,1:T(8,128)(2,1)S(1)} %bitcast.75), kind=kOutput, calls=%fused_computation.56.clone.1 | convolution fusion | flops 281020416 | bytes 17965056 | tf_op jit(solution)/shard_map/while/body/eval_jaxpr/sub | solution.py:65
  264.4 8.5 %fusion.47 = bf16[8,32,256]{2,1,0:T(8,128)(2,1)S(1)} fusion(bf16[2048,8,32]{0,2,1:T(8,128)(2,1)S(1)} %bitcast.74, f32[8,256,2048]{2,1,0:T(8,128)} %get-tuple-element.99, f32[8,256]{1,0:T(8,128)S(1)} %get-tuple-element.100), kind=kOutput, calls=%fused_computation.11.clone.1 | convolution fusion | flops 276889600 | bytes 17965056 | tf_op jit(solution)/shard_map/while/body/eval_jaxpr/hqk,khd->qhd/dot_general | solution.py:67
  273.6 10.1 %all_to_all.24 = bf16[2,512,256]{2,1,0:T(8,128)(2,1)S(1)} all-to-all(bf16[2,512,256]{2,1,0:T(8,128)(2,1)} %bitcast.90), channel_id=1, replica_groups=mesh['seq'=16,'head'=2] {'head'}, dimensions={0} | all-to-all | bytes 1048576 | tf_op jit(solution)/shard_map/all_to_all | solution.py:129
  (68 shorter events, 25.9 us)
Async XLA Ops:
  0.0 283.9 %copy-start = (bf16[512,512]{1,0:T(8,128)(2,1)S(1)}, bf16[512,512]{1,0:T(8,128)(2,1)}, u32[]{:S(2)}) copy-start(bf16[512,512]{1,0:T(8,128)(2,1)} %param.10) | copy-start | bytes 1572868
  0.0 7.1 %copy-start.2 = (s32[64,8]{0,1:T(8,128)S(1)}, s32[64,8]{0,1:T(8,128)}, u32[]{:S(2)}) copy-start(s32[64,8]{0,1:T(8,128)} %param.11) | copy-start | bytes 6148
  2.6 13.8 %collective-permute-start = (bf16[1,512,512]{2,1,0:T(8,128)(2,1)S(1)}, bf16[1,512,512]{2,1,0:T(8,128)(2,1)}, u32[]{:S(2)}, u32[]{:S(2)}) collective-permute-start(bf16[1,512,512]{2,1,0:T(8,128)(2,1)S(1)} %get-tuple-element.65), channel_id=1, source_target_pairs={{0,1},{1,0},{2,3},{3,2},{4,5},{5,4},{6,7},{7,6},{8,9},{9,8},{10,11... | collective-permute-start | bytes 1572872 | tf_op jit(solution)/shard_map/ppermute | solution.py:26
  19.9 1.2 copy-start.1
  26.7 132.7 %all-to-all-start = ((bf16[16,1,256,512]{3,2,1,0:T(8,128)(2,1)}), bf16[16,1,256,512]{3,2,1,0:T(8,128)(2,1)}, u32[]{:S(2)}, u32[]{:S(2)}) async-start(bf16[16,1,256,512]{3,2,1,0:T(8,128)(2,1)} %bitcast.78), calls=%async_computation | async-start | bytes 8388608 | tf_op jit(solution)/shard_map/all_to_all | solution.py:116
  32.9 103.8 %collective-permute-start.1 = (bf16[4,256,512]{2,1,0:T(8,128)(2,1)S(1)}, bf16[4,256,512]{2,1,0:T(8,128)(2,1)S(1)}, u32[]{:S(2)}, u32[]{:S(2)}) collective-permute-start(bf16[4,256,512]{2,1,0:T(8,128)(2,1)S(1)} %bitcast.80), channel_id=1, source_target_pairs={{0,2},{2,4},{4,6},{6,8},{8,10},{10,12},{12,14},{14,16},{16,18},{18... | collective-permute-start | bytes 3145736 | tf_op jit(solution)/shard_map/ppermute | solution.py:45
  34.9 101.8 %collective-permute-start.2 = (bf16[4,256,512]{2,1,0:T(8,128)(2,1)S(1)}, bf16[4,256,512]{2,1,0:T(8,128)(2,1)}, u32[]{:S(2)}, u32[]{:S(2)}) collective-permute-start(bf16[4,256,512]{2,1,0:T(8,128)(2,1)S(1)} %bitcast.81), channel_id=1, source_target_pairs={{2,0},{4,2},{6,4},{8,6},{10,8},{12,10},{14,12},{16,14},{18,16},{20... | collective-permute-start | bytes 3145736 | tf_op jit(solution)/shard_map/ppermute | solution.py:47
  181.1 13.5 %slice-start = ((bf16[1024,768]{1,0:T(8,128)(2,1)}), bf16[1024,256]{1,0:T(8,128)(2,1)S(1)}, s32[]{:S(2)}) async-start(bf16[1024,768]{1,0:T(8,128)(2,1)} %copy-done.1), calls=%async_computation.2 | async-start | bytes 1048576 | tf_op jit(solution)/shard_map/slice | solution.py:91
